TPU v7x, 32 devices: a whole 2x2x4 slice. The times are simulated.
32 devices in a mesh: dp: 8 (over z, y), fsdp: 4 (over x, core).
Axes of the slice: x: 2, y: 2, z: 4, core: 2. Of those that a mesh axis runs over, the one named last changes fastest.
Arguments:
- keys: bfloat16 [256, 8, 896], P(('dp', 'fsdp')), may hold values from -8 to 8
- residual: bfloat16 [256, 8, 896], P(('dp', 'fsdp')), may hold values from -6 to 6
- se_reduce: bfloat16 [896, 224], P('fsdp'), may hold values from -0.625 to 0.625
- se_expand: bfloat16 [896, 224], P('fsdp'), may hold values from -1.25 to 1.25
- conv_weight: bfloat16 [3, 896, 896], P(None, 'fsdp'), may hold values from -0.1875 to 0.1875
- bn_gain: float32 [896], replicated, may hold values from 0.1 to 1.9
- bn_bias: float32 [896], replicated, may hold values from -3 to 3
- shuffle: int32 [256], P(('dp', 'fsdp')), may hold values from 0 to 63, as said below
- unshuffle: int32 [256], P(('dp', 'fsdp')), may hold values from 0 to 63, as said below
Outputs:
- encoded: bfloat16 [256, 8, 896], P(('dp', 'fsdp'))
Inputs may be any that keep to these rules, and one draw needn't show every extreme that they name: `shuffle`: A permutation of the 64 positions within each group of devices sharing an fsdp index (positions ordered by dp index, then by image); each device sends exactly 1 of its images to every device of its group. `unshuffle`: the inverse of shuffle within each group.
All inputs are finite; a program needn't handle non-finite values.
Results may differ from a plain program's by a relative error of at most 0.013.
Values may be sent and summed in bfloat16 or wider, within the bound.
A program may use at most 64 MiB of HBM per device.

v0:
```python
import jax
import jax.numpy as jnp
from jax import lax
from jax.sharding import PartitionSpec as P

epsilon = 1e-05


def project_rows(flat, weight_rows):
    return jnp.dot(
        flat,
        lax.all_gather(weight_rows, "fsdp", axis=0, tiled=True),
        preferred_element_type=jnp.float32,
    )


def encode_block(batch_block, reduce_full, expand_full, conv_weight):
    images, positions, channels = batch_block.shape
    layers = conv_weight.shape[0]
    flat = batch_block.reshape(images * positions, channels)
    for layer in range(layers - 1):
        flat = jax.nn.relu(project_rows(flat, conv_weight[layer])).astype(jnp.bfloat16)
    entry = flat.reshape(images, positions, channels)
    pooled = jnp.mean(entry, axis=1, dtype=jnp.float32).astype(jnp.bfloat16)
    squeeze_act = jax.nn.relu(
        jnp.dot(pooled, reduce_full, preferred_element_type=jnp.float32)
    ).astype(jnp.bfloat16)
    excite = jax.nn.sigmoid(
        lax.dot_general(
            squeeze_act, expand_full, (((1,), (1,)), ((), ())), preferred_element_type=jnp.float32
        )
    )
    scaled = (entry * excite[:, None, :]).astype(jnp.bfloat16).reshape(images * positions, channels)
    projected = project_rows(scaled, conv_weight[layers - 1])
    return projected.reshape(images, positions, channels)


def local(keys, residual, se_reduce, se_expand, conv_weight, bn_gain, bn_bias, shuffle, unshuffle):
    images, positions, channels = keys.shape
    count = images * positions
    reduce_full, expand_full = (
        lax.all_gather(se_reduce, "fsdp", axis=0, tiled=True),
        lax.all_gather(se_expand, "fsdp", axis=0, tiled=True),
    )
    send_order = jnp.argsort(shuffle)
    back_order = jnp.argsort(send_order)
    outgoing = jnp.take(keys, send_order, axis=0)
    arrived = lax.all_to_all(outgoing, "dp", split_axis=0, concat_axis=0, tiled=True)
    projected = encode_block(arrived, reduce_full, expand_full, conv_weight)
    row_sums = jnp.sum(projected, axis=(0, 1))
    square_sums = jnp.sum(projected * projected, axis=(0, 1))
    mean_rows = row_sums / count
    variance = square_sums / count - mean_rows * mean_rows
    scale_rows = lax.rsqrt(variance + epsilon) * bn_gain
    normed_here = ((projected - mean_rows) * scale_rows + bn_bias).astype(jnp.bfloat16)
    returned = lax.all_to_all(normed_here, "dp", split_axis=0, concat_axis=0, tiled=True)
    normed = jnp.take(returned, back_order, axis=0)
    encoded = jax.nn.relu(normed.astype(jnp.float32) + residual.astype(jnp.float32))
    return encoded.astype(jnp.bfloat16)


def solution(mesh):
    placed = (
        P(("dp", "fsdp"), None, None),
        P(("dp", "fsdp"), None, None),
        P("fsdp", None),
        P("fsdp", None),
        P(None, "fsdp", None),
        P(),
        P(),
        P(("dp", "fsdp")),
        P(("dp", "fsdp")),
    )
    return jax.shard_map(
        local, mesh=mesh, in_specs=placed, out_specs=P(("dp", "fsdp"), None, None), check_vma=False
    )
```

profile of v0, /device:TPU:0, one launch (start us, length us, event | category | flops | bytes accessed | tf_op | source)
XLA Modules:
  0.0 100.1 jit_solution(3672770266905854364)
XLA Ops:
  6.5 0.0 copy-start
  6.5 0.0 copy-start.6
  6.5 0.0 copy-start.1
  6.5 0.0 all-gather.7.cloned.1.call-start
  6.5 2.4 %fusion.42 = (bf16[1,224,896]{2,1,0:T(8,128)(2,1)}, bf16[1,224,896]{2,1,0:T(8,128)(2,1)}, bf16[1,224,896]{2,1,0:T(8,128)(2,1)}) fusion(bf16[3,224,896]{2,1,0:T(8,128)(2,1)} %param.15), kind=kLoop, calls=%fused_computation.45 | loop fusion | bytes 2408448 | tf_op jit(solution)/shard_map/slice | solution.py:22
  8.9 0.0 copy-start.2
  8.9 0.0 all-gather.7.cloned.1.call-update
  9.0 0.0 all-gather.9.cloned.1.call-start
  9.0 0.7 all-gather.9.cloned.1.call-update
  9.7 0.0 all-gather.11.cloned.1.call-start
  9.8 0.7 all-gather.11.cloned.1.call-update
  10.5 0.0 copy-done.6
  10.5 1.0 sort.31
  11.5 0.0 copy-done
  11.5 0.6 gather_fusion
  12.0 0.7 broadcast_select_fusion
  12.8 7.3 %all-to-all-start = ((bf16[8,8,896]{2,1,0:T(8,128)(2,1)}), bf16[8,8,896]{2,1,0:T(8,128)(2,1)S(1)}, u32[]{:S(2)}, u32[]{:S(2)}) async-start(bf16[8,8,896]{2,1,0:T(8,128)(2,1)} %broadcast_select_fusion), calls=%async_computation | async-start | bytes 229376 | tf_op jit(solution)/shard_map/all_to_all | solution.py:48
  20.1 1.0 sort.32
  21.1 0.0 copy-done.1
  21.1 9.7 %all_gather.17 = bf16[896,224]{1,0:T(8,128)(2,1)S(1)} all-gather(bf16[224,224]{1,0:T(8,128)(2,1)S(1)} %copy-done.1), channel_id=1, replica_groups=mesh['dp'=8,'fsdp'=4] {'fsdp'}, dimensions={0}, use_global_device_ids=true | all-gather | bytes 501760 | tf_op jit(solution)/shard_map/all_gather | solution.py:42
  30.8 0.0 copy-done.2
  30.8 6.9 %all_gather.18 = bf16[896,224]{1,0:T(8,128)(2,1)S(1)} all-gather(bf16[224,224]{1,0:T(8,128)(2,1)S(1)} %copy-done.2), channel_id=1, replica_groups=mesh['dp'=8,'fsdp'=4] {'fsdp'}, dimensions={0}, use_global_device_ids=true | all-gather | bytes 501760 | tf_op jit(solution)/shard_map/all_gather | solution.py:43
  37.7 0.0 all-to-all-done
  37.7 0.0 all-gather.7.cloned.1.call-done
  37.7 17.8 %all-gather.9.cloned.1.call-done = bf16[1,896,896]{2,1,0:T(8,128)(2,1)} async-done(((bf16[1,224,896]{2,1,0:T(8,128)(2,1)}), bf16[1,896,896]{2,1,0:T(8,128)(2,1)}) %all-gather.9.cloned.1.call-update) | async-done | bytes 1605648 | tf_op jit(solution)/shard_map/all_gather | solution.py:12
  55.6 2.6 %bitcast_reduce_fusion = (f32[8,896]{1,0:T(8,128)S(1)}, f32[64,896]{1,0:T(8,128)S(1)}) fusion(bf16[1,896,896]{2,1,0:T(8,128)(2,1)} %all-gather.9.cloned.1.call-done, bf16[1,896,896]{2,1,0:T(8,128)(2,1)} %all-gather.7.cloned.1.call-done, bf16[8,8,896]{2,1,0:T(8,128)(2,1)S(1)} %all-to-all-done), kind=kOutput, calls=%fused_computation.21 | convolution fusion | flops 205857792 | bytes 3584000 | tf_op jit(solution)/shard_map/dot_general | solution.py:10
  58.2 0.0 copy-start.5
  58.2 0.0 copy-start.4
  58.2 0.4 fusion.25
  58.6 0.0 copy-start.3
  58.6 18.4 %all-gather.11.cloned.1.call-done = bf16[1,896,896]{2,1,0:T(8,128)(2,1)} async-done(((bf16[1,224,896]{2,1,0:T(8,128)(2,1)}), bf16[1,896,896]{2,1,0:T(8,128)(2,1)}) %all-gather.11.cloned.1.call-update) | async-done | bytes 1605648 | tf_op jit(solution)/shard_map/all_gather | solution.py:12
  77.0 1.8 %fusion.41 = (f32[896]{0:T(1024)S(1)}, f32[896]{0:T(1024)S(1)}, f32[8,8,896]{2,1,0:T(8,128)S(1)}) fusion(bf16[1,896,896]{2,1,0:T(8,128)(2,1)} %all-gather.11.cloned.1.call-done, f32[64,896]{1,0:T(8,128)S(1)} %get-tuple-element.18, f32[8,896]{1,0:T(8,128)S(1)} %fusion.25), kind=kOutput, calls=%fused_computation.44 | convolution fusion | flops 103045376 | bytes 2100224 | tf_op jit(solution)/shard_map/dot_general | solution.py:10
  78.8 0.0 copy-done.5
  78.8 0.0 copy-done.4
  78.8 0.7 add_convert_fusion
  79.5 5.5 %all-to-all-start.1 = ((bf16[8,8,896]{2,1,0:T(8,128)(2,1)}), bf16[8,8,896]{2,1,0:T(8,128)(2,1)S(1)}, u32[]{:S(2)}, u32[]{:S(2)}) async-start(bf16[8,8,896]{2,1,0:T(8,128)(2,1)} %add_convert_fusion), calls=%async_computation.1 | async-start | bytes 229376 | tf_op jit(solution)/shard_map/all_to_all | solution.py:56
  85.0 7.2 %all-to-all-done.1 = bf16[8,8,896]{2,1,0:T(8,128)(2,1)S(1)} async-done(((bf16[8,8,896]{2,1,0:T(8,128)(2,1)}), bf16[8,8,896]{2,1,0:T(8,128)(2,1)S(1)}, u32[]{:S(2)}, u32[]{:S(2)}) %all-to-all-start.1) | async-done | bytes 114720 | tf_op jit(solution)/shard_map/all_to_all | solution.py:56
  92.3 0.6 gather_fusion.1
  92.8 0.0 copy-done.3
  92.8 0.8 maximum_convert_fusion
  (9 shorter events, 0.1 us)
Async XLA Ops:
  6.5 4.9 %copy-start = (bf16[8,8,896]{2,1,0:T(8,128)(2,1)S(1)}, bf16[8,8,896]{2,1,0:T(8,128)(2,1)}, u32[]{:S(2)}) copy-start(bf16[8,8,896]{2,1,0:T(8,128)(2,1)} %param.11) | copy-start | bytes 344068
  6.5 3.9 %copy-start.6 = (s32[8]{0:T(128)S(1)}, s32[8]{0:T(128)}, u32[]{:S(2)}) copy-start(s32[8]{0:T(128)} %param.18) | copy-start | bytes 100
  6.5 14.5 %copy-start.1 = (bf16[224,224]{1,0:T(8,128)(2,1)S(1)}, bf16[224,224]{1,0:T(8,128)(2,1)}, u32[]{:S(2)}) copy-start(bf16[224,224]{1,0:T(8,128)(2,1)} %param.13) | copy-start | bytes 301060
  6.5 31.2 %all-gather.7.cloned.1.call-start = ((), (), s32[]{:S(2)}) async-start(), calls=%async_computation.2 | async-start | bytes 2007040 | tf_op jit(solution)/shard_map/all_gather | solution.py:12
  8.9 21.8 %copy-start.2 = (bf16[224,224]{1,0:T(8,128)(2,1)S(1)}, bf16[224,224]{1,0:T(8,128)(2,1)}, u32[]{:S(2)}) copy-start(bf16[224,224]{1,0:T(8,128)(2,1)} %param.14) | copy-start | bytes 301060
  9.0 46.6 %all-gather.9.cloned.1.call-start = ((), (), s32[]{:S(2)}) async-start(), calls=%async_computation.3 | async-start | bytes 2007040 | tf_op jit(solution)/shard_map/all_gather | solution.py:12
  9.7 67.3 %all-gather.11.cloned.1.call-start = ((), (), s32[]{:S(2)}) async-start(), calls=%async_computation.4 | async-start | bytes 2007040 | tf_op jit(solution)/shard_map/all_gather | solution.py:12
  12.8 24.9 %all-to-all-start = ((bf16[8,8,896]{2,1,0:T(8,128)(2,1)}), bf16[8,8,896]{2,1,0:T(8,128)(2,1)S(1)}, u32[]{:S(2)}, u32[]{:S(2)}) async-start(bf16[8,8,896]{2,1,0:T(8,128)(2,1)} %broadcast_select_fusion), calls=%async_computation | async-start | bytes 229376 | tf_op jit(solution)/shard_map/all_to_all | solution.py:48
  58.2 20.6 %copy-start.5 = (f32[896]{0:T(1024)S(1)}, f32[896]{0:T(1024)}, u32[]{:S(2)}) copy-start(f32[896]{0:T(1024)} %param.16) | copy-start | bytes 10756
  58.2 20.6 %copy-start.4 = (f32[896]{0:T(1024)S(1)}, f32[896]{0:T(1024)}, u32[]{:S(2)}) copy-start(f32[896]{0:T(1024)} %param.17) | copy-start | bytes 10756
  58.6 34.2 %copy-start.3 = (bf16[8,8,896]{2,1,0:T(8,128)(2,1)S(1)}, bf16[8,8,896]{2,1,0:T(8,128)(2,1)}, u32[]{:S(2)}) copy-start(bf16[8,8,896]{2,1,0:T(8,128)(2,1)} %param.12) | copy-start | bytes 344068
  79.5 12.8 %all-to-all-start.1 = ((bf16[8,8,896]{2,1,0:T(8,128)(2,1)}), bf16[8,8,896]{2,1,0:T(8,128)(2,1)S(1)}, u32[]{:S(2)}, u32[]{:S(2)}) async-start(bf16[8,8,896]{2,1,0:T(8,128)(2,1)} %add_convert_fusion), calls=%async_computation.1 | async-start | bytes 229376 | tf_op jit(solution)/shard_map/all_to_all | solution.py:56
Sparse Core Ops, SparseCore 0:
  9.1 24.9 all-gather.6
  35.7 19.8 all-gather.8
  57.1 19.8 all-gather.10
where the time goes:
time: 100 us
  waiting for transfers between devices  44.8 us (45%)
  blocking collectives  16.6 us (17%)
  between operations  13.2 us (13%)
  starting transfers between devices  12.9 us (13%)
  matrix products  4.83 us (5%)
  other arithmetic  4.17 us (4%)
  local copies, waits for them, and re-layouts  3.57 us (4%)
    all_gather x3, waiting for transfers between devices, project_rows(): lax.all_gather(weight_rows, 'fsdp', axis=0, tiled=True)  36.2 us
    all_gather x1, blocking collectives, local(): lax.all_gather(se_reduce, 'fsdp', axis=0, tiled=True)  9.71 us
    all_to_all x1, starting transfers between devices, local(): lax.all_to_all(outgoing, 'dp', split_axis=0, concat_axis=0, tiled=True)  7.28 us
    all_to_all x1, waiting for transfers between devices, local(): lax.all_to_all(normed_here, 'dp', split_axis=0, concat_axis=0, tiled=True)  7.23 us
    all_gather x1, blocking collectives, local(): lax.all_gather(se_expand, 'fsdp', axis=0, tiled=True)  6.94 us
    all_to_all x1, starting transfers between devices, local(): lax.all_to_all(normed_here, 'dp', split_axis=0, concat_axis=0, tiled=True)  5.52 us
    dot_general x2, matrix products, project_rows(): jnp.dot(flat, lax.all_gather(weight_rows, 'fsdp', axis=0, tiled=True), pr...  4.4 us
    slice x1, local copies, waits for them, and re-layouts, encode_block(): conv_weight[layer]  2.4 us
  transfers between devices with their start and end apart: 5, of which 3 were waited for; matrix products, arithmetic and copies ran while one was open for 6% of the time, Pallas kernels for 0%

commit v1 on v0

--- a/solution.py
+++ b/solution.py
@@ -7,11 +7,32 @@
 
 
 def project_rows(flat, weight_rows):
-    return jnp.dot(
-        flat,
-        lax.all_gather(weight_rows, "fsdp", axis=0, tiled=True),
-        preferred_element_type=jnp.float32,
-    )
+
+    def slot_lead(w_in, array_axis):
+        r_now, g_now, part_next = (
+            lax.axis_size("fsdp"),
+            lax.axis_index("fsdp"),
+            w_in.shape[array_axis],
+        )
+        v_now = lax.dynamic_update_slice_in_dim(
+            jnp.zeros(
+                tuple((pp * r_now if s == array_axis else pp for s, pp in enumerate(w_in.shape))),
+                w_in.dtype,
+            ),
+            w_in,
+            g_now * part_next,
+            axis=array_axis,
+        )
+        ix = 1
+        while ix < r_now:
+            w_in = lax.ppermute(w_in, "fsdp", tuple(((s, (s + 1) % r_now) for s in range(r_now))))
+            v_now = lax.dynamic_update_slice_in_dim(
+                v_now, w_in, (g_now - ix) % r_now * part_next, axis=array_axis
+            )
+            ix = ix + 1
+        return v_now
+
+    return jnp.dot(flat, slot_lead(weight_rows, 0), preferred_element_type=jnp.float32)
 
 
 def encode_block(batch_block, reduce_full, expand_full, conv_weight):

time: 100 us -> 80.4 us (0.80)
  waiting for transfers between devices: 44.8 us -> 18.3 us
  local copies, waits for them, and re-layouts: 3.57 us -> 17.2 us
  between operations: 13.2 us -> 0.21 us
  starting transfers between devices: 12.9 us -> 16.2 us
  blocking collectives: 16.6 us -> 18.2 us
    all_gather x3 -> x0, waiting for transfers between devices: 36.2 us -> none  [project_rows(): lax.all_gather(weight_rows, 'fsdp', axis=0, tiled=True)]
    dynamic_update_slice x0 -> x12, local copies, waits for them, and re-layouts: none -> 11.5 us  [the longest x9 9.65 us: slot_lead(): lax.dynamic_update_slice_in_dim(v_now, w_in, (g_now - ix) % r_now * part_...]
    ppermute x0 -> x9, waiting for transfers between devices: none -> 11.1 us  [slot_lead(): lax.ppermute(w_in, 'fsdp', tuple(((s, (s + 1) % r_now) for s in range(r_n...]
    ppermute x0 -> x9, starting transfers between devices: none -> 4.33 us  [slot_lead(): lax.ppermute(w_in, 'fsdp', tuple(((s, (s + 1) % r_now) for s in range(r_n...]
    all_gather x1, blocking collectives: 6.94 us -> 10.6 us  [local(): lax.all_gather(se_expand, 'fsdp', axis=0, tiled=True)]
    slice x1 -> x0, local copies, waits for them, and re-layouts: 2.4 us -> none  [encode_block(): conv_weight[layer]]
    squeeze x0 -> x1, local copies, waits for them, and re-layouts: none -> 2.32 us  [encode_block(): conv_weight[layer]]
    all_gather x1, blocking collectives: 9.71 us -> 7.64 us  [local(): lax.all_gather(se_reduce, 'fsdp', axis=0, tiled=True)]
  transfers between devices with their start and end apart: 5 -> 11, of which waited for: 3 -> 5; matrix products, arithmetic and copies ran while one was open for 6% -> 25% of each run, Pallas kernels for 0% -> 0%
where the time goes in v1:
time: 80.4 us; the launch traced here: 79.7 us
  waiting for transfers between devices  18.3 us (23%)
  blocking collectives  18.2 us (23%)
  local copies, waits for them, and re-layouts  17.2 us (21%)
  starting transfers between devices  16.2 us (20%)
  matrix products  4.78 us (6%)
  other arithmetic  4.76 us (6%)
    ppermute x9, waiting for transfers between devices, slot_lead(): lax.ppermute(w_in, 'fsdp', tuple(((s, (s + 1) % r_now) for s in range(r_n...  11.1 us
    all_gather x1, blocking collectives, local(): lax.all_gather(se_expand, 'fsdp', axis=0, tiled=True)  10.6 us
    dynamic_update_slice x9, local copies, waits for them, and re-layouts, slot_lead(): lax.dynamic_update_slice_in_dim(v_now, w_in, (g_now - ix) % r_now * part_...  9.65 us
    all_gather x1, blocking collectives, local(): lax.all_gather(se_reduce, 'fsdp', axis=0, tiled=True)  7.64 us
    all_to_all x1, waiting for transfers between devices, local(): lax.all_to_all(normed_here, 'dp', split_axis=0, concat_axis=0, tiled=True)  7.21 us
    all_to_all x1, starting transfers between devices, local(): lax.all_to_all(normed_here, 'dp', split_axis=0, concat_axis=0, tiled=True)  6 us
    all_to_all x1, starting transfers between devices, local(): lax.all_to_all(outgoing, 'dp', split_axis=0, concat_axis=0, tiled=True)  5.83 us
    ppermute x9, starting transfers between devices, slot_lead(): lax.ppermute(w_in, 'fsdp', tuple(((s, (s + 1) % r_now) for s in range(r_n...  4.33 us
  transfers between devices with their start and end apart: 11, of which 5 were waited for; matrix products, arithmetic and copies ran while one was open for 25% of the time, Pallas kernels for 0%

profile of v1, /device:TPU:0, one launch (start us, length us, event | category | flops | bytes accessed | tf_op | source)
XLA Modules:
  0.0 79.7 jit_solution(5614869759038604212)
XLA Ops:
  0.0 2.3 %slice_bitcast_fusion.2 = (bf16[224,896]{1,0:T(8,128)(2,1)}, bf16[224,896]{1,0:T(8,128)(2,1)}, bf16[224,896]{1,0:T(8,128)(2,1)}) fusion(bf16[3,224,896]{2,1,0:T(8,128)(2,1)} %param.15), kind=kLoop, calls=%fused_computation.17 | loop fusion | bytes 2408448 | tf_op jit(solution)/shard_map/squeeze | solution.py:43
  2.3 0.5 collective-permute-start.3
  2.8 2.6 %collective-permute-start = (bf16[224,896]{1,0:T(8,128)(2,1)}, bf16[224,896]{1,0:T(8,128)(2,1)}, u32[]{:S(2)}, u32[]{:S(2)}) collective-permute-start(bf16[224,896]{1,0:T(8,128)(2,1)} %get-tuple-element.12), channel_id=1, source_target_pairs={{0,1},{1,2},{2,3},{3,0},{4,5},{5,6},{6,7},{7,4},{8,9},{9,10},{10,1... | collective-permute-start | bytes 1204232 | tf_op jit(solution)/shard_map/ppermute | solution.py:28
  5.4 1.0 %sort.31 = (s32[8]{0:T(128)}, s32[8]{0:T(128)S(1)}) sort(s32[8]{0:T(128)S(1)} %copy-done.7, s32[8]{0:T(128)S(1)} %iota.7), dimensions={0}, to_apply=%region_0.0 | sort | flops 24 | bytes 128 | tf_op jit(solution)/shard_map/jit(argsort)/sort | solution.py:66
  6.4 0.6 gather_fusion
  7.0 0.7 broadcast_select_fusion
  7.7 5.8 %all-to-all-start = ((bf16[8,8,896]{2,1,0:T(8,128)(2,1)}), bf16[8,8,896]{2,1,0:T(8,128)(2,1)}, u32[]{:S(2)}, u32[]{:S(2)}) async-start(bf16[8,8,896]{2,1,0:T(8,128)(2,1)} %broadcast_select_fusion), calls=%async_computation | async-start | bytes 229376 | tf_op jit(solution)/shard_map/all_to_all | solution.py:69
  13.5 0.0 collective-permute-start.6
  13.5 0.1 broadcast.36.clone.1
  13.7 0.0 copy-start.2
  13.8 1.3 %broadcast.36.clone.2 = bf16[896,896]{1,0:T(8,128)(2,1)} broadcast(bf16[]{:T(256)} %constant.68.clone.1), dimensions={} | broadcast | bytes 1605634 | tf_op jit(solution)/shard_map/broadcast.13
  15.0 0.8 constant_dynamic-update-slice_fusion.11
  15.8 1.0 %sort.32 = (s32[8]{0:T(128)}, s32[8]{0:T(128)S(1)}) sort(s32[8]{0:T(128)S(1)} %get-tuple-element.8, s32[8]{0:T(128)S(1)} %iota.8), dimensions={0}, to_apply=%region_4.6 | sort | flops 24 | bytes 128 | tf_op jit(solution)/shard_map/jit(argsort)/sort | solution.py:67
  16.8 0.5 copy-done.8
  17.4 7.6 %all_gather.6 = bf16[896,224]{1,0:T(8,128)(2,1)} all-gather(bf16[224,224]{1,0:T(8,128)(2,1)S(1)} %copy-done.2), channel_id=1, replica_groups=mesh['dp'=8,'fsdp'=4] {'fsdp'}, dimensions={0}, use_global_device_ids=true | all-gather | bytes 501760 | tf_op jit(solution)/shard_map/all_gather | solution.py:63
  25.0 0.1 broadcast.36.clone
  25.1 1.0 %constant_dynamic-update-slice_fusion.3 = bf16[896,896]{1,0:T(8,128)(2,1)S(1)} fusion(bf16[896,896]{1,0:T(8,128)(2,1)S(1)} %broadcast.36.clone, s32[]{:T(128)S(6)} %select_n.54, bf16[3,224,896]{2,1,0:T(8,128)(2,1)} %param.15), kind=kLoop, calls=%fused_computation.38 | loop fusion | bytes 802820 | tf_op jit(solution)/shard_map/dynamic_update_slice | solution.py:17
  26.2 0.0 collective-permute-done.3
  26.2 0.4 collective-permute-start.4
  26.6 10.6 %all_gather.7 = bf16[896,224]{1,0:T(8,128)(2,1)} all-gather(bf16[224,224]{1,0:T(8,128)(2,1)S(1)} %copy-done.3), channel_id=1, replica_groups=mesh['dp'=8,'fsdp'=4] {'fsdp'}, dimensions={0}, use_global_device_ids=true | all-gather | bytes 501760 | tf_op jit(solution)/shard_map/all_gather | solution.py:64
  37.2 0.2 collective-permute-start.1
  37.3 0.6 collective-permute-start.7
  37.9 0.6 pad_clamp_fusion
  38.5 1.0 %constant_dynamic-update-slice_fusion.6 = bf16[896,896]{1,0:T(8,128)(2,1)S(1)} fusion(bf16[896,896]{1,0:T(8,128)(2,1)S(1)} %constant_dynamic-update-slice_fusion.7, bf16[224,896]{1,0:T(8,128)(2,1)} %collective-permute-done.3, s32[]{:T(128)S(6)} %select_n.56), kind=kLoop, calls=%fused_computation.41 | loop fusion | bytes 802820 | tf_op jit(solution)/shard_map/dynamic_update_slice | solution.py:29
  39.5 1.8 %constant_dynamic-update-slice_fusion.10 = bf16[896,896]{1,0:T(8,128)(2,1)} fusion(bf16[896,896]{1,0:T(8,128)(2,1)} %constant_dynamic-update-slice_fusion.11, bf16[224,896]{1,0:T(8,128)(2,1)} %collective-permute-done, s32[]{:T(128)S(6)} %select_n.56), kind=kLoop, calls=%fused_computation.45 | loop fusion | bytes 802820 | tf_op jit(solution)/shard_map/dynamic_update_slice | solution.py:29
  41.3 0.0 collective-permute-done.4
  41.3 0.2 collective-permute-start.5
  41.5 1.0 %constant_dynamic-update-slice_fusion.2 = bf16[896,896]{1,0:T(8,128)(2,1)S(1)} fusion(bf16[896,896]{1,0:T(8,128)(2,1)S(1)} %constant_dynamic-update-slice_fusion.3, bf16[224,896]{1,0:T(8,128)(2,1)} %collective-permute-done.6, s32[]{:T(128)S(6)} %select_n.56), kind=kLoop, calls=%fused_computation.37 | loop fusion | bytes 802820 | tf_op jit(solution)/shard_map/dynamic_update_slice | solution.py:29
  42.5 2.2 %collective-permute-done.1 = bf16[224,896]{1,0:T(8,128)(2,1)} collective-permute-done((bf16[224,896]{1,0:T(8,128)(2,1)}, bf16[224,896]{1,0:T(8,128)(2,1)}, u32[]{:S(2)}, u32[]{:S(2)}) %collective-permute-start.1) | collective-permute-done | bytes 401440 | tf_op jit(solution)/shard_map/ppermute | solution.py:28
  44.8 4.3 %collective-permute-done.7 = bf16[224,896]{1,0:T(8,128)(2,1)} collective-permute-done((bf16[224,896]{1,0:T(8,128)(2,1)}, bf16[224,896]{1,0:T(8,128)(2,1)}, u32[]{:S(2)}, u32[]{:S(2)}) %collective-permute-start.7) | collective-permute-done | bytes 401440 | tf_op jit(solution)/shard_map/ppermute | solution.py:28
  49.1 1.0 %constant_dynamic-update-slice_fusion.5 = bf16[896,896]{1,0:T(8,128)(2,1)S(1)} fusion(bf16[896,896]{1,0:T(8,128)(2,1)S(1)} %constant_dynamic-update-slice_fusion.6, bf16[224,896]{1,0:T(8,128)(2,1)} %collective-permute-done.4, s32[]{:T(128)S(6)} %select_n.58), kind=kLoop, calls=%fused_computation.40 | loop fusion | bytes 802820 | tf_op jit(solution)/shard_map/dynamic_update_slice | solution.py:29
  50.1 1.8 %constant_dynamic-update-slice_fusion.9 = bf16[896,896]{1,0:T(8,128)(2,1)} fusion(bf16[896,896]{1,0:T(8,128)(2,1)} %constant_dynamic-update-slice_fusion.10, bf16[224,896]{1,0:T(8,128)(2,1)} %collective-permute-done.1, s32[]{:T(128)S(6)} %select_n.58), kind=kLoop, calls=%fused_computation.44 | loop fusion | bytes 802820 | tf_op jit(solution)/shard_map/dynamic_update_slice | solution.py:29
  51.9 1.0 %constant_dynamic-update-slice_fusion.1 = bf16[896,896]{1,0:T(8,128)(2,1)S(1)} fusion(bf16[896,896]{1,0:T(8,128)(2,1)S(1)} %constant_dynamic-update-slice_fusion.2, bf16[224,896]{1,0:T(8,128)(2,1)} %collective-permute-done.7, s32[]{:T(128)S(6)} %select_n.58), kind=kLoop, calls=%fused_computation.36 | loop fusion | bytes 802820 | tf_op jit(solution)/shard_map/dynamic_update_slice | solution.py:29
  53.0 0.3 collective-permute-done.5
  53.3 4.3 %collective-permute-done.2 = bf16[224,896]{1,0:T(8,128)(2,1)S(1)} collective-permute-done((bf16[224,896]{1,0:T(8,128)(2,1)}, bf16[224,896]{1,0:T(8,128)(2,1)S(1)}, u32[]{:S(2)}, u32[]{:S(2)}) %collective-permute-start.2) | collective-permute-done | bytes 401440 | tf_op jit(solution)/shard_map/ppermute | solution.py:28
  57.6 0.8 constant_dynamic-update-slice_fusion.8
  58.4 2.8 %bitcast_reduce_fusion = (f32[8,896]{1,0:T(8,128)}, f32[64,896]{1,0:T(8,128)S(1)}) fusion(bf16[896,896]{1,0:T(8,128)(2,1)S(1)} %constant_dynamic-update-slice_fusion.4, bf16[896,896]{1,0:T(8,128)(2,1)} %constant_dynamic-update-slice_fusion.8, bf16[8,8,896]{2,1,0:T(8,128)(2,1)} %all-to-all-done), kind=kOutput, calls=%fused_computation.20 | convolution fusion | flops 205857792 | bytes 3584000 | tf_op jit(solution)/shard_map/dot_general | solution.py:35
  61.2 1.6 %fusion.7 = f32[8,896]{1,0:T(8,128)S(1)} fusion(bf16[896,224]{1,0:T(8,128)(2,1)} %all_gather.7, bf16[896,224]{1,0:T(8,128)(2,1)} %all_gather.6, f32[8,896]{1,0:T(8,128)} %get-tuple-element.17), kind=kOutput, calls=%fused_computation.12 | convolution fusion | flops 6461952 | bytes 860160 | tf_op jit(solution)/shard_map/dot_general | solution.py:50
  62.8 0.0 copy-start.5
  62.8 0.0 copy-start.9
  62.8 1.1 %constant_dynamic-update-slice_fusion = bf16[896,896]{1,0:T(8,128)(2,1)S(1)} fusion(bf16[896,896]{1,0:T(8,128)(2,1)S(1)} %constant_dynamic-update-slice_fusion.1, bf16[224,896]{1,0:T(8,128)(2,1)} %collective-permute-done.8, s32[]{:T(128)S(6)} %select_n.60), kind=kLoop, calls=%fused_computation.35 | loop fusion | bytes 802820 | tf_op jit(solution)/shard_map/dynamic_update_slice | solution.py:29
  63.9 0.0 copy-start.4
  63.9 0.4 fusion.23
  64.3 0.7 add_convert_fusion
  65.0 6.0 %all-to-all-start.1 = ((bf16[8,8,896]{2,1,0:T(8,128)(2,1)}), bf16[8,8,896]{2,1,0:T(8,128)(2,1)S(1)}, u32[]{:S(2)}, u32[]{:S(2)}) async-start(bf16[8,8,896]{2,1,0:T(8,128)(2,1)} %add_convert_fusion), calls=%async_computation.1 | async-start | bytes 229376 | tf_op jit(solution)/shard_map/all_to_all | solution.py:77
  71.0 7.2 %all-to-all-done.1 = bf16[8,8,896]{2,1,0:T(8,128)(2,1)S(1)} async-done(((bf16[8,8,896]{2,1,0:T(8,128)(2,1)}), bf16[8,8,896]{2,1,0:T(8,128)(2,1)S(1)}, u32[]{:S(2)}, u32[]{:S(2)}) %all-to-all-start.1) | async-done | bytes 114720 | tf_op jit(solution)/shard_map/all_to_all | solution.py:77
  78.2 0.7 gather_fusion.1
  78.9 0.8 maximum_convert_fusion
  (31 shorter events, 0.2 us)
Async XLA Ops:
  0.0 6.4 %copy-start = (bf16[8,8,896]{2,1,0:T(8,128)(2,1)S(1)}, bf16[8,8,896]{2,1,0:T(8,128)(2,1)}, u32[]{:S(2)}) copy-start(bf16[8,8,896]{2,1,0:T(8,128)(2,1)} %param.11) | copy-start | bytes 344068
  0.0 5.4 %copy-start.7 = (s32[8]{0:T(128)S(1)}, s32[8]{0:T(128)}, u32[]{:S(2)}) copy-start(s32[8]{0:T(128)} %param.18) | copy-start | bytes 100
  2.3 11.3 %copy-start.1 = (bf16[3,224,896]{2,1,0:T(8,128)(2,1)S(1)}, bf16[3,224,896]{2,1,0:T(8,128)(2,1)}, u32[]{:S(2)}) copy-start(bf16[3,224,896]{2,1,0:T(8,128)(2,1)} %param.15) | copy-start | bytes 3612676
  2.3 23.9 %collective-permute-start.3 = (bf16[224,896]{1,0:T(8,128)(2,1)}, bf16[224,896]{1,0:T(8,128)(2,1)}, u32[]{:S(2)}, u32[]{:S(2)}) collective-permute-start(bf16[224,896]{1,0:T(8,128)(2,1)} %get-tuple-element.14), channel_id=1, source_target_pairs={{0,1},{1,2},{2,3},{3,0},{4,5},{5,6},{6,7},{7,4},{8,9},{9,10},{10,1... | collective-permute-start | bytes 1204232 | tf_op jit(solution)/shard_map/ppermute | solution.py:28
  2.8 34.4 %collective-permute-start = (bf16[224,896]{1,0:T(8,128)(2,1)}, bf16[224,896]{1,0:T(8,128)(2,1)}, u32[]{:S(2)}, u32[]{:S(2)}) collective-permute-start(bf16[224,896]{1,0:T(8,128)(2,1)} %get-tuple-element.12), channel_id=1, source_target_pairs={{0,1},{1,2},{2,3},{3,0},{4,5},{5,6},{6,7},{7,4},{8,9},{9,10},{10,1... | collective-permute-start | bytes 1204232 | tf_op jit(solution)/shard_map/ppermute | solution.py:28
  7.7 50.7 %all-to-all-start = ((bf16[8,8,896]{2,1,0:T(8,128)(2,1)}), bf16[8,8,896]{2,1,0:T(8,128)(2,1)}, u32[]{:S(2)}, u32[]{:S(2)}) async-start(bf16[8,8,896]{2,1,0:T(8,128)(2,1)} %broadcast_select_fusion), calls=%async_computation | async-start | bytes 229376 | tf_op jit(solution)/shard_map/all_to_all | solution.py:69
  13.5 23.8 %collective-permute-start.6 = (bf16[224,896]{1,0:T(8,128)(2,1)}, bf16[224,896]{1,0:T(8,128)(2,1)}, u32[]{:S(2)}, u32[]{:S(2)}) collective-permute-start(bf16[224,896]{1,0:T(8,128)(2,1)} %get-tuple-element.13), channel_id=1, source_target_pairs={{0,1},{1,2},{2,3},{3,0},{4,5},{5,6},{6,7},{7,4},{8,9},{9,10},{10,1... | collective-permute-start | bytes 1204232 | tf_op jit(solution)/shard_map/ppermute | solution.py:28
  13.7 3.7 %copy-start.2 = (bf16[224,224]{1,0:T(8,128)(2,1)S(1)}, bf16[224,224]{1,0:T(8,128)(2,1)}, u32[]{:S(2)}) copy-start(bf16[224,224]{1,0:T(8,128)(2,1)} %param.13) | copy-start | bytes 301060
  15.8 10.8 %copy-start.3 = (bf16[224,224]{1,0:T(8,128)(2,1)S(1)}, bf16[224,224]{1,0:T(8,128)(2,1)}, u32[]{:S(2)}) copy-start(bf16[224,224]{1,0:T(8,128)(2,1)} %param.14) | copy-start | bytes 301060
  16.8 0.5 copy-start.8
  26.2 15.1 %collective-permute-start.4 = (bf16[224,896]{1,0:T(8,128)(2,1)}, bf16[224,896]{1,0:T(8,128)(2,1)}, u32[]{:S(2)}, u32[]{:S(2)}) collective-permute-start(bf16[224,896]{1,0:T(8,128)(2,1)} %collective-permute-done.3), channel_id=1, source_target_pairs={{0,1},{1,2},{2,3},{3,0},{4,5},{5,6},{6,7},{7,4},{8,9},{9,10},{10,1... | collective-permute-start | bytes 1204232 | tf_op jit(solution)/shard_map/ppermute | solution.py:28
  37.2 7.6 %collective-permute-start.1 = (bf16[224,896]{1,0:T(8,128)(2,1)}, bf16[224,896]{1,0:T(8,128)(2,1)}, u32[]{:S(2)}, u32[]{:S(2)}) collective-permute-start(bf16[224,896]{1,0:T(8,128)(2,1)} %collective-permute-done), channel_id=1, source_target_pairs={{0,1},{1,2},{2,3},{3,0},{4,5},{5,6},{6,7},{7,4},{8,9},{9,10},{10,1... | collective-permute-start | bytes 1204232 | tf_op jit(solution)/shard_map/ppermute | solution.py:28
  37.3 11.7 %collective-permute-start.7 = (bf16[224,896]{1,0:T(8,128)(2,1)}, bf16[224,896]{1,0:T(8,128)(2,1)}, u32[]{:S(2)}, u32[]{:S(2)}) collective-permute-start(bf16[224,896]{1,0:T(8,128)(2,1)} %collective-permute-done.6), channel_id=1, source_target_pairs={{0,1},{1,2},{2,3},{3,0},{4,5},{5,6},{6,7},{7,4},{8,9},{9,10},{10,1... | collective-permute-start | bytes 1204232 | tf_op jit(solution)/shard_map/ppermute | solution.py:28
  41.3 11.9 %collective-permute-start.5 = (bf16[224,896]{1,0:T(8,128)(2,1)}, bf16[224,896]{1,0:T(8,128)(2,1)S(1)}, u32[]{:S(2)}, u32[]{:S(2)}) collective-permute-start(bf16[224,896]{1,0:T(8,128)(2,1)} %collective-permute-done.4), channel_id=1, source_target_pairs={{0,1},{1,2},{2,3},{3,0},{4,5},{5,6},{6,7},{7,4},{8,9},{9,10},{10,1... | collective-permute-start | bytes 1204232 | tf_op jit(solution)/shard_map/ppermute | solution.py:28
  44.8 12.8 %collective-permute-start.2 = (bf16[224,896]{1,0:T(8,128)(2,1)}, bf16[224,896]{1,0:T(8,128)(2,1)S(1)}, u32[]{:S(2)}, u32[]{:S(2)}) collective-permute-start(bf16[224,896]{1,0:T(8,128)(2,1)} %collective-permute-done.1), channel_id=1, source_target_pairs={{0,1},{1,2},{2,3},{3,0},{4,5},{5,6},{6,7},{7,4},{8,9},{9,10},{10,1... | collective-permute-start | bytes 1204232 | tf_op jit(solution)/shard_map/ppermute | solution.py:28
  49.1 13.7 %collective-permute-start.8 = (bf16[224,896]{1,0:T(8,128)(2,1)}, bf16[224,896]{1,0:T(8,128)(2,1)}, u32[]{:S(2)}, u32[]{:S(2)}) collective-permute-start(bf16[224,896]{1,0:T(8,128)(2,1)} %collective-permute-done.7), channel_id=1, source_target_pairs={{0,1},{1,2},{2,3},{3,0},{4,5},{5,6},{6,7},{7,4},{8,9},{9,10},{10,1... | collective-permute-start | bytes 1204232 | tf_op jit(solution)/shard_map/ppermute | solution.py:28
  62.8 1.5 %copy-start.6 = (f32[896]{0:T(1024)S(1)}, f32[896]{0:T(1024)}, u32[]{:S(2)}) copy-start(f32[896]{0:T(1024)} %param.16) | copy-start | bytes 10756
  62.8 1.5 %copy-start.5 = (f32[896]{0:T(1024)S(1)}, f32[896]{0:T(1024)}, u32[]{:S(2)}) copy-start(f32[896]{0:T(1024)} %param.17) | copy-start | bytes 10756
  62.8 8.2 %copy-start.9 = (s32[8]{0:T(128)S(1)}, s32[8]{0:T(128)}, u32[]{:S(2)}) copy-start(s32[8]{0:T(128)} %copy-done.8) | copy-start | bytes 100
  63.9 15.0 %copy-start.4 = (bf16[8,8,896]{2,1,0:T(8,128)(2,1)S(1)}, bf16[8,8,896]{2,1,0:T(8,128)(2,1)}, u32[]{:S(2)}) copy-start(bf16[8,8,896]{2,1,0:T(8,128)(2,1)} %param.12) | copy-start | bytes 344068
  65.0 13.2 %all-to-all-start.1 = ((bf16[8,8,896]{2,1,0:T(8,128)(2,1)}), bf16[8,8,896]{2,1,0:T(8,128)(2,1)S(1)}, u32[]{:S(2)}, u32[]{:S(2)}) async-start(bf16[8,8,896]{2,1,0:T(8,128)(2,1)} %add_convert_fusion), calls=%async_computation.1 | async-start | bytes 229376 | tf_op jit(solution)/shard_map/all_to_all | solution.py:77
